TPU v7x, 256 devices: a whole 4x4x8 slice. The times are simulated.
256 devices in a mesh: row: 16 (over z_hi, y, core), col: 16 (over z_lo, x).
Axes of the slice: x: 4, y: 4, z: 8 (z_hi: 2, z_lo: 4; z = z_hi * 4 + z_lo), core: 2. Of those that a mesh axis runs over, the one named last changes fastest.
Arguments:
- features: float32 [131072, 256], P(('row', 'col')), may hold values from -6 to 6
- self_weight: float32 [256, 128], replicated, may hold values from -0.375 to 0.375
- neigh_weight: float32 [256, 128], replicated, may hold values from -0.75 to 0.75
- out_bias: float32 [128], replicated, may hold values from -3 to 3
- adjacency_tiles: int32 [1024, 32, 128, 128], P('row', 'col'), may hold values from 0 to 3, as said below
- tile_columns: int32 [1024, 32], P('row', 'col'), may hold values from 0 to 63
- live_counts: int32 [1024, 16], P('row', 'col'), may hold values from 1 to 2, as said below
- cotangent: float32 [131072, 128], P(('row', 'col')), may hold values from -6 to 6
Outputs:
- hidden_out: float32 [131072, 128], P(('row', 'col'))
- grad_features: float32 [131072, 256], P(('row', 'col'))
- grad_self: float32 [256, 128], replicated
- grad_neigh: float32 [256, 128], replicated
- grad_bias: float32 [128], replicated
Inputs may be any that keep to these rules, and one draw needn't show every extreme that they name: `adjacency_tiles`: edge multiplicities; most entries are zero. `live_counts`: slots at or after this count in a tile-row's block are ignored, whatever they hold.
All inputs are finite; a program needn't handle non-finite values.
Results may differ from a plain program's by a relative error of at most 0.0003.
Values sent between devices are 32-bit elements; how exact they have to be, the bound alone decides.
A program may use at most 128 MiB of HBM per device.

v0:
```python
import math
import jax
import jax.numpy as jnp
from jax import lax
from jax.sharding import PartitionSpec as P


def live_weights(tile_values, count_block):
    slot_ids = jnp.arange(tile_values.shape[1], dtype=jnp.int32)
    live_slots = (slot_ids[None, :] < count_block).astype(jnp.float32)
    return tile_values.astype(jnp.float32) * live_slots[:, :, None, None]


def forward_tiles(weighted, column_block, source):
    tile_size = weighted.shape[2]
    feature_width = source.shape[1]
    source_tiles = source.reshape(-1, tile_size, feature_width)
    picked = source_tiles[column_block]
    products = jnp.einsum("tkab,tkbw->taw", weighted, picked, precision=lax.Precision.HIGHEST)
    return products.reshape(-1, feature_width)


def backward_tiles(weighted, column_block, source, col_tiles):
    tile_size = weighted.shape[2]
    feature_width = source.shape[1]
    source_tiles = source.reshape(-1, tile_size, feature_width)
    spread = jnp.einsum("tkab,taw->tkbw", weighted, source_tiles, precision=lax.Precision.HIGHEST)
    merged = jax.ops.segment_sum(
        spread.reshape(-1, tile_size, feature_width),
        column_block.reshape(-1),
        num_segments=col_tiles,
    )
    return merged.reshape(-1, feature_width)


def local(
    features,
    self_weight,
    neigh_weight,
    out_bias,
    adjacency_tiles,
    tile_columns,
    live_counts,
    cotangent,
):
    highest = lax.Precision.HIGHEST
    weighted = live_weights(adjacency_tiles, live_counts)
    degree_part = jnp.sum(weighted, axis=(1, 3)).reshape(-1)
    local_self = jnp.dot(features, self_weight, precision=highest)
    gathered = lax.all_gather(features, "row", axis=0, tiled=True)
    partial_rows = forward_tiles(weighted, tile_columns, gathered)
    summed, degree_sum = (
        lax.psum_scatter(partial_rows, "col", scatter_dimension=0, tiled=True),
        lax.psum_scatter(degree_part, "col", scatter_dimension=0, tiled=True),
    )
    degree = 1.0 + degree_sum
    aggregated = summed / degree[:, None]
    pre_act = local_self + jnp.dot(aggregated, neigh_weight, precision=highest) + out_bias
    hidden_out = jax.nn.silu(pre_act)
    sig_value = jax.nn.sigmoid(pre_act)
    grad_pre = cotangent * sig_value * (1.0 + pre_act * (1.0 - sig_value))
    scaled = grad_pre / degree[:, None]
    block_rows = lax.all_gather(scaled, "col", axis=0, tiled=True)
    col_tiles = features.shape[0] * lax.axis_size("row") // adjacency_tiles.shape[2]
    back_part = backward_tiles(weighted, tile_columns, block_rows, col_tiles)
    back_rows = lax.psum_scatter(back_part, "row", scatter_dimension=0, tiled=True)
    grad_features = jnp.dot(grad_pre, self_weight.T, precision=highest) + jnp.dot(
        back_rows, neigh_weight.T, precision=highest
    )
    grad_self_part = jnp.dot(features.T, grad_pre, precision=highest)
    grad_neigh_part = jnp.dot(aggregated.T, grad_pre, precision=highest)
    grad_bias_part = jnp.sum(grad_pre, axis=0)
    totals = lax.psum((grad_self_part, grad_neigh_part, grad_bias_part), ("row", "col"))
    node_total = features.shape[0] * lax.axis_size("row") * lax.axis_size("col")
    factor = 1.0 / math.sqrt(node_total)
    return (hidden_out, grad_features, totals[0] * factor, totals[1] * factor, totals[2] * factor)


def solution(mesh):
    return jax.shard_map(
        local,
        mesh=mesh,
        in_specs=(
            P(("row", "col"), None),
            P(),
            P(),
            P(),
            P("row", "col", None, None),
            P("row", "col"),
            P("row", "col"),
            P(("row", "col"), None),
        ),
        out_specs=(P(("row", "col"), None), P(("row", "col"), None), P(), P(), P()),
        check_vma=False,
    )
```

profile of v0, /device:TPU:2, one launch (start us, length us, event | category | flops | bytes accessed | tf_op | source)
XLA Modules:
  0.0 724.2 jit_solution(1517068199887440945)
XLA Ops:
  7.2 0.7 all-gather.3.cloned.1.call-update
  8.0 0.7 compare_select_fusion
  8.9 0.7 fusion.8
  9.6 112.4 %all-gather.3.cloned.1.call-done = f32[8192,256]{1,0:T(8,128)} async-done(((f32[512,256]{1,0:T(8,128)}), f32[8192,256]{1,0:T(8,128)}) %all-gather.3.cloned.1.call-update) | async-done | bytes 8388624 | tf_op jit(solution)/shard_map/all_gather | solution.py:50
  122.0 13.2 %gather_fusion = f32[128,128,256]{2,1,0:T(8,128)} fusion(f32[64,128,256]{2,1,0:T(8,128)} %bitcast.33, s32[1024]{0:T(1024)S(1)} %pad_clamp_fusion), kind=kCustom, calls=%fused_computation | custom fusion | bytes 33554944 | tf_op jit(solution)/shard_map/gather | solution.py:18
  135.3 22.8 %fusion.2 = f32[64,128,256,1]{2,1,3,0:T(8,128)} fusion(f32[64,2,128,256]{3,2,1,0:T(8,128)} %bitcast.30, s32[64,2,128,128]{3,2,1,0:T(8,128)} %param.12, f32[64,2]{1,0:T(8,128)S(1)} %fusion.8), kind=kOutput, calls=%fused_computation.5 | convolution fusion | flops 6446645248 | bytes 33554944 | tf_op jit(solution)/shard_map/tkab,tkbw->taw/dot_general | solution.py:19
  160.0 5.1 fusion.1
  165.1 71.6 %all-reduce = f32[8192]{0:T(1024)S(1)} all-reduce(f32[8192]{0:T(1024)S(1)} %bitcast.36), channel_id=3, replica_groups=mesh['row'=16,'col'=16] {'col'}, use_global_device_ids=true, to_apply=%region_2.0.clone | all-reduce | flops 8192 | bytes 65536
  237.3 21.3 %reduce-scatter.3.cloned.1.call-done = f32[512,256]{1,0:T(8,128)} async-done(((f32[8192,256]{1,0:T(8,128)}), f32[512,256]{1,0:T(8,128)}) %reduce-scatter.3.cloned.1.call-update) | async-done | bytes 524304 | tf_op jit(solution)/shard_map/reduce_scatter | solution.py:53
  258.6 2.4 fusion.9
  261.0 0.8 broadcast_divide_fusion.1
  262.3 1.3 convolution_bitcast_fusion
  263.6 2.4 fusion.7
  266.1 82.5 %all-gather.5.cloned.1.call-done = f32[8192,128]{1,0:T(8,128)} async-done(((f32[512,128]{1,0:T(8,128)}), f32[8192,128]{1,0:T(8,128)}) %all-gather.5.cloned.1.call-update) | async-done | bytes 4194320 | tf_op jit(solution)/shard_map/all_gather | solution.py:63
  348.6 19.8 %fusion = f32[64,2,128,128]{3,2,1,0:T(8,128)} fusion(f32[64,128,128,1]{2,1,3,0:T(8,128)} %bitcast.35, s32[64,2,128,128]{3,2,1,0:T(8,128)} %param.12, f32[64,2]{1,0:T(8,128)S(1)} %fusion.8), kind=kOutput, calls=%fused_computation.3 | convolution fusion | flops 3225419776 | bytes 20972032 | tf_op jit(solution)/shard_map/tkab,taw->tkbw/dot_general | solution.py:27
  368.4 2.5 broadcast_in_dim.5
  370.8 26.9 %scatter_fusion = f32[64,128,128]{2,1,0:T(8,128)} fusion(f32[64,128,128]{2,1,0:T(8,128)} %broadcast_in_dim.5, s32[128]{0:T(128)S(1)} %reshape.69, f32[128,128,128]{2,1,0:T(8,128)} %bitcast.34), kind=kCustom, calls=%fused_computation.1 | custom fusion | flops 2097152 | bytes 25166336 | tf_op jit(solution)/shard_map/scatter-add | solution.py:28
  397.8 75.4 %psum.23 = f32[128]{0:T(128)S(1)} all-reduce(f32[128]{0:T(128)S(1)} %get-tuple-element.22), channel_id=1, replica_groups=mesh['row'=16,'col'=16] {'row','col'}, use_global_device_ids=true, to_apply=%region_8.9 | all-reduce | flops 128 | bytes 1024 | tf_op jit(solution)/shard_map/psum | solution.py:73
  474.2 133.8 %all-reduce.4.cloned.1.call-done = (f32[256,128]{0,1:T(8,128)}, f32[256,128]{0,1:T(8,128)}) async-done(((f32[256,128]{0,1:T(8,128)}, f32[256,128]{0,1:T(8,128)}), (f32[256,128]{0,1:T(8,128)}, f32[256,128]{0,1:T(8,128)})) %all-reduce.4.cloned.1.call-update) | async-done | bytes 262160 | tf_op jit(solution)/shard_map/psum | solution.py:73
  608.1 1.0 broadcast_multiply_fusion
  609.1 0.8 copy.29
  609.8 0.8 copy.30
  610.6 104.8 %reduce-scatter.5.cloned.1.call-done = f32[512,128]{1,0:T(8,128)} async-done(((f32[8192,128]{1,0:T(8,128)}), f32[512,128]{1,0:T(8,128)}) %reduce-scatter.5.cloned.1.call-update) | async-done | bytes 262160 | tf_op jit(solution)/shard_map/reduce_scatter | solution.py:66
  715.4 2.3 convolution_add_fusion
  (33 shorter events, 3.8 us)
Async XLA Ops:
  7.2 251.4 %copy-start = (f32[256,128]{1,0:T(8,128)S(1)}, f32[256,128]{1,0:T(8,128)}, u32[]{:S(2)}) copy-start(f32[256,128]{1,0:T(8,128)} %param.10) | copy-start | bytes 393220
  7.2 114.9 %all-gather.3.cloned.1.call-start = ((), (), s32[]{:S(2)}) async-start(), calls=%async_computation.2 | async-start | bytes 8912896 | tf_op jit(solution)/shard_map/all_gather | solution.py:50
  7.9 250.7 %reduce-scatter.3.cloned.1.call-start = ((), (), s32[]{:S(2)}) async-start(), calls=%async_computation.3 | async-start | bytes 8912896 | tf_op jit(solution)/shard_map/reduce_scatter | solution.py:53
  158.1 0.7 copy-start.6
  158.1 78.6 %copy-start.1 = (f32[512,256]{1,0:T(8,128)S(1)}, f32[512,256]{1,0:T(8,128)}, u32[]{:S(2)}) copy-start(f32[512,256]{1,0:T(8,128)} %param.8) | copy-start | bytes 1572868
  158.1 78.6 %copy-start.2 = (f32[256,128]{1,0:T(8,128)S(1)}, f32[256,128]{1,0:T(8,128)}, u32[]{:S(2)}) copy-start(f32[256,128]{1,0:T(8,128)} %param.9) | copy-start | bytes 393220
  158.1 100.5 %copy-start.4 = (f32[512,128]{1,0:T(8,128)S(1)}, f32[512,128]{1,0:T(8,128)}, u32[]{:S(2)}) copy-start(f32[512,128]{1,0:T(8,128)} %param.15) | copy-start | bytes 786436
  158.1 100.5 %copy-start.5 = (f32[128]{0:T(128)S(1)}, f32[128]{0:T(128)}, u32[]{:S(2)}) copy-start(f32[128]{0:T(128)} %param.11) | copy-start | bytes 1540
  158.2 103.9 %copy-start.3 = (s32[64,2]{0,1:T(2,128)S(1)}, s32[64,2]{0,1:T(2,128)}, u32[]{:S(2)}) copy-start(s32[64,2]{0,1:T(2,128)} %param.13) | copy-start | bytes 1540
  158.2 190.4 %all-gather.5.cloned.1.call-start = ((), (), s32[]{:S(2)}) async-start(), calls=%async_computation.4 | async-start | bytes 4456448 | tf_op jit(solution)/shard_map/all_gather | solution.py:63
  261.9 346.2 %all-reduce.4.cloned.1.call-start = ((), (), s32[]{:S(2)}) async-start(), calls=%async_computation.6 | async-start | bytes 524288 | tf_op jit(solution)/shard_map/psum | solution.py:73
  266.0 449.3 %reduce-scatter.5.cloned.1.call-start = ((), (), s32[]{:S(2)}) async-start(), calls=%async_computation.5 | async-start | bytes 4456448 | tf_op jit(solution)/shard_map/reduce_scatter | solution.py:66
Sparse Core Ops, SparseCore 0:
  10.7 111.2 all-gather.2
  158.3 100.2 reduce-scatter.2
  262.0 86.5 all-gather.4
  354.6 253.3 all-reduce.3
  612.2 103.0 reduce-scatter.4
where the time goes:
time: 725 us; the launch traced here: 724 us
  waiting for transfers between devices  456 us (63%)
  blocking collectives  147 us (20%)
  matrix products  52.1 us (7%)
  other arithmetic  35.8 us (5%)
  local copies, waits for them, and re-layouts  18.9 us (3%)
  between operations  14.5 us (2%)
    psum x1, waiting for transfers between devices, local(): lax.psum((grad_self_part, grad_neigh_part, grad_bias_part), ('row', 'col'))  134 us
    all_gather x1, waiting for transfers between devices, local(): gathered = lax.all_gather(features, 'row', axis=0, tiled=True)  112 us
    reduce_scatter x1, waiting for transfers between devices, local(): lax.psum_scatter(back_part, 'row', scatter_dimension=0, tiled=True)  105 us
    all_gather x1, waiting for transfers between devices, local(): block_rows = lax.all_gather(scaled, 'col', axis=0, tiled=True)  82.5 us
    psum x1, blocking collectives, local(): lax.psum((grad_self_part, grad_neigh_part, grad_bias_part), ('row', 'col'))  75.4 us
    unnamed x1, blocking collectives  71.6 us
    scatter-add x1, other arithmetic, backward_tiles(): jax.ops.segment_sum(spread.reshape(-1, tile_size, feature_width), column_...  26.9 us
    dot_general x1, matrix products, forward_tiles(): jnp.einsum('tkab,tkbw->taw', weighted, picked, precision=lax.Precision.HI...  22.8 us
  transfers between devices with their start and end apart: 5, of which 5 were waited for; matrix products, arithmetic and copies ran while one was open for 9% of the time, Pallas kernels for 0%

commit v1 on v0

--- a/solution.py
+++ b/solution.py
@@ -60,7 +60,11 @@
     sig_value = jax.nn.sigmoid(pre_act)
     grad_pre = cotangent * sig_value * (1.0 + pre_act * (1.0 - sig_value))
     scaled = grad_pre / degree[:, None]
-    block_rows = lax.all_gather(scaled, "col", axis=0, tiled=True)
+    _build_levels_all = lambda page: jnp.concatenate(
+        jax.lax.all_to_all(jnp.stack([page for _ in range(jax.lax.axis_size("col"))]), "col", 0, 0),
+        axis=0,
+    )
+    block_rows = _build_levels_all(scaled)
     col_tiles = features.shape[0] * lax.axis_size("row") // adjacency_tiles.shape[2]
     back_part = backward_tiles(weighted, tile_columns, block_rows, col_tiles)
     back_rows = lax.psum_scatter(back_part, "row", scatter_dimension=0, tiled=True)

time: 725 us -> 665 us (0.917)
  waiting for transfers between devices: 456 us -> 373 us
  blocking collectives: 147 us -> 161 us
  starting transfers between devices: 0.38 us -> 7.74 us
    all_gather x1 -> x0, waiting for transfers between devices: 82.5 us -> none  [local(): block_rows = lax.all_gather(scaled, 'col', axis=0, tiled=True)]
    all_to_all x0 -> x1, waiting for transfers between devices: none -> 69 us  [local(): jax.lax.all_to_all(jnp.stack([page for _ in range(jax.lax.axis_size('col'...]
    psum x1, waiting for transfers between devices: 134 us -> 65.1 us  [local(): lax.psum((grad_self_part, grad_neigh_part, grad_bias_part), ('row', 'col'))]
    psum x1, blocking collectives: 75.4 us -> 89.6 us  [local(): lax.psum((grad_self_part, grad_neigh_part, grad_bias_part), ('row', 'col'))]
    all_to_all x0 -> x1, starting transfers between devices: none -> 7.41 us  [local(): jax.lax.all_to_all(jnp.stack([page for _ in range(jax.lax.axis_size('col'...]
  transfers between devices with their start and end apart: 5 -> 5, of which waited for: 5 -> 5; matrix products, arithmetic and copies ran while one was open for 9% -> 10% of each run, Pallas kernels for 0% -> 0%
where the time goes in v1:
time: 665 us; the launch traced here: 664 us
  waiting for transfers between devices  373 us (56%)
  blocking collectives  161 us (24%)
  matrix products  51.2 us (8%)
  other arithmetic  35.1 us (5%)
  local copies, waits for them, and re-layouts  21.3 us (3%)
  between operations  14.5 us (2%)
  starting transfers between devices  7.74 us (1%)
    all_gather x1, waiting for transfers between devices, local(): gathered = lax.all_gather(features, 'row', axis=0, tiled=True)  112 us
    reduce_scatter x1, waiting for transfers between devices, local(): lax.psum_scatter(back_part, 'row', scatter_dimension=0, tiled=True)  105 us
    psum x1, blocking collectives, local(): lax.psum((grad_self_part, grad_neigh_part, grad_bias_part), ('row', 'col'))  89.6 us
    unnamed x1, blocking collectives  71.6 us
    all_to_all x1, waiting for transfers between devices, local(): jax.lax.all_to_all(jnp.stack([page for _ in range(jax.lax.axis_size('col'...  69 us
    psum x1, waiting for transfers between devices, local(): lax.psum((grad_self_part, grad_neigh_part, grad_bias_part), ('row', 'col'))  65.1 us
    scatter-add x1, other arithmetic, backward_tiles(): jax.ops.segment_sum(spread.reshape(-1, tile_size, feature_width), column_...  26.9 us
    dot_general x1, matrix products, forward_tiles(): jnp.einsum('tkab,tkbw->taw', weighted, picked, precision=lax.Precision.HI...  22.8 us
  transfers between devices with their start and end apart: 5, of which 5 were waited for; matrix products, arithmetic and copies ran while one was open for 10% of the time, Pallas kernels for 0%

profile of v1, /device:TPU:2, one launch (start us, length us, event | category | flops | bytes accessed | tf_op | source)
XLA Modules:
  0.0 664.1 jit_solution(15552702959407788897)
XLA Ops:
  8.0 0.7 compare_select_fusion
  8.9 0.7 fusion.8
  9.6 112.4 %all-gather.2.cloned.1.call-done = f32[8192,256]{1,0:T(8,128)} async-done(((f32[512,256]{1,0:T(8,128)}), f32[8192,256]{1,0:T(8,128)}) %all-gather.2.cloned.1.call-update) | async-done | bytes 8388624 | tf_op jit(solution)/shard_map/all_gather | solution.py:50
  122.0 13.2 %gather_fusion = f32[128,128,256]{2,1,0:T(8,128)} fusion(f32[64,128,256]{2,1,0:T(8,128)} %bitcast.33, s32[1024]{0:T(1024)S(1)} %pad_clamp_fusion), kind=kCustom, calls=%fused_computation | custom fusion | bytes 33554944 | tf_op jit(solution)/shard_map/gather | solution.py:18
  135.3 22.8 %fusion.2 = f32[64,128,256,1]{2,1,3,0:T(8,128)} fusion(f32[64,2,128,256]{3,2,1,0:T(8,128)} %bitcast.30, s32[64,2,128,128]{3,2,1,0:T(8,128)} %param.12, f32[64,2]{1,0:T(8,128)S(1)} %fusion.8), kind=kOutput, calls=%fused_computation.5 | convolution fusion | flops 6446645248 | bytes 33554944 | tf_op jit(solution)/shard_map/tkab,tkbw->taw/dot_general | solution.py:19
  160.0 5.1 fusion.1
  165.1 71.6 %all-reduce = f32[8192]{0:T(1024)S(1)} all-reduce(f32[8192]{0:T(1024)S(1)} %bitcast.35), channel_id=3, replica_groups=mesh['row'=16,'col'=16] {'col'}, use_global_device_ids=true, to_apply=%region_2.0.clone | all-reduce | flops 8192 | bytes 65536
  237.3 21.3 %reduce-scatter.3.cloned.1.call-done = f32[512,256]{1,0:T(8,128)} async-done(((f32[8192,256]{1,0:T(8,128)}), f32[512,256]{1,0:T(8,128)}) %reduce-scatter.3.cloned.1.call-update) | async-done | bytes 524304 | tf_op jit(solution)/shard_map/reduce_scatter | solution.py:53
  258.6 2.5 fusion.9
  261.2 2.3 stack.2
  263.6 7.4 %all-to-all-start = ((f32[16,512,128]{2,1,0:T(8,128)}), f32[16,512,128]{2,1,0:T(8,128)}, u32[]{:S(2)}, u32[]{:S(2)}) async-start(f32[16,512,128]{2,1,0:T(8,128)} %stack.2), calls=%async_computation.1 | async-start | bytes 8388608 | tf_op jit(solution)/shard_map/all_to_all | solution.py:64
  271.4 1.3 convolution_bitcast_fusion
  272.7 1.4 fusion.7
  274.1 69.0 %all-to-all-done = f32[16,512,128]{2,1,0:T(8,128)} async-done(((f32[16,512,128]{2,1,0:T(8,128)}), f32[16,512,128]{2,1,0:T(8,128)}, u32[]{:S(2)}, u32[]{:S(2)}) %all-to-all-start) | async-done | bytes 4194336 | tf_op jit(solution)/shard_map/all_to_all | solution.py:64
  343.1 19.8 %fusion = f32[64,2,128,128]{3,2,1,0:T(8,128)} fusion(f32[64,128,128,1]{2,1,3,0:T(8,128)} %bitcast.9, s32[64,2,128,128]{3,2,1,0:T(8,128)} %param.12, f32[64,2]{1,0:T(8,128)S(1)} %fusion.8), kind=kOutput, calls=%fused_computation.3 | convolution fusion | flops 3225419776 | bytes 20972032 | tf_op jit(solution)/shard_map/tkab,taw->tkbw/dot_general | solution.py:27
  362.9 2.5 broadcast_in_dim.5
  365.4 26.9 %scatter_fusion = f32[64,128,128]{2,1,0:T(8,128)} fusion(f32[64,128,128]{2,1,0:T(8,128)} %broadcast_in_dim.5, s32[128]{0:T(128)S(1)} %reshape.67, f32[128,128,128]{2,1,0:T(8,128)} %bitcast.34), kind=kCustom, calls=%fused_computation.1 | custom fusion | flops 2097152 | bytes 25166336 | tf_op jit(solution)/shard_map/scatter-add | solution.py:28
  392.2 89.6 %psum.23 = f32[128]{0:T(128)S(1)} all-reduce(f32[128]{0:T(128)S(1)} %get-tuple-element.22), channel_id=1, replica_groups=mesh['row'=16,'col'=16] {'row','col'}, use_global_device_ids=true, to_apply=%region_8.9 | all-reduce | flops 128 | bytes 1024 | tf_op jit(solution)/shard_map/psum | solution.py:77
  482.9 65.1 %all-reduce.4.cloned.1.call-done = (f32[256,128]{0,1:T(8,128)}, f32[256,128]{0,1:T(8,128)}) async-done(((f32[256,128]{0,1:T(8,128)}, f32[256,128]{0,1:T(8,128)}), (f32[256,128]{0,1:T(8,128)}, f32[256,128]{0,1:T(8,128)})) %all-reduce.4.cloned.1.call-update) | async-done | bytes 262160 | tf_op jit(solution)/shard_map/psum | solution.py:77
  548.0 1.0 broadcast_multiply_fusion
  549.0 0.8 copy.29
  549.7 0.8 copy.30
  550.5 104.8 %reduce-scatter.5.cloned.1.call-done = f32[512,128]{1,0:T(8,128)} async-done(((f32[8192,128]{1,0:T(8,128)}), f32[512,128]{1,0:T(8,128)}) %reduce-scatter.5.cloned.1.call-update) | async-done | bytes 262160 | tf_op jit(solution)/shard_map/reduce_scatter | solution.py:70
  655.3 2.3 convolution_add_fusion
  (35 shorter events, 4.7 us)
Async XLA Ops:
  7.2 251.4 %copy-start = (f32[256,128]{1,0:T(8,128)S(1)}, f32[256,128]{1,0:T(8,128)}, u32[]{:S(2)}) copy-start(f32[256,128]{1,0:T(8,128)} %param.10) | copy-start | bytes 393220
  7.2 114.9 %all-gather.2.cloned.1.call-start = ((), (), s32[]{:S(2)}) async-start(), calls=%async_computation.3 | async-start | bytes 8912896 | tf_op jit(solution)/shard_map/all_gather | solution.py:50
  7.9 250.7 %reduce-scatter.3.cloned.1.call-start = ((), (), s32[]{:S(2)}) async-start(), calls=%async_computation.4 | async-start | bytes 8912896 | tf_op jit(solution)/shard_map/reduce_scatter | solution.py:53
  158.1 0.7 copy-start.7
  158.1 78.6 %copy-start.1 = (f32[512,256]{1,0:T(8,128)S(1)}, f32[512,256]{1,0:T(8,128)}, u32[]{:S(2)}) copy-start(f32[512,256]{1,0:T(8,128)} %param.8) | copy-start | bytes 1572868
  158.1 78.6 %copy-start.2 = (f32[256,128]{1,0:T(8,128)S(1)}, f32[256,128]{1,0:T(8,128)}, u32[]{:S(2)}) copy-start(f32[256,128]{1,0:T(8,128)} %param.9) | copy-start | bytes 393220
  158.1 100.5 %copy-start.5 = (f32[512,128]{1,0:T(8,128)S(1)}, f32[512,128]{1,0:T(8,128)}, u32[]{:S(2)}) copy-start(f32[512,128]{1,0:T(8,128)} %param.15) | copy-start | bytes 786436
  158.1 100.5 %copy-start.6 = (f32[128]{0:T(128)S(1)}, f32[128]{0:T(128)}, u32[]{:S(2)}) copy-start(f32[128]{0:T(128)} %param.11) | copy-start | bytes 1540
  237.3 33.9 %copy-start.3 = (s32[64,2]{0,1:T(2,128)S(1)}, s32[64,2]{0,1:T(2,128)}, u32[]{:S(2)}) copy-start(s32[64,2]{0,1:T(2,128)} %param.13) | copy-start | bytes 1540
  258.6 14.1 %copy-start.4 = (f32[512,256]{1,0:T(8,128)S(1)}, f32[512,256]{1,0:T(8,128)}, u32[]{:S(2)}) copy-start(f32[512,256]{1,0:T(8,128)} %reduce-scatter.3.cloned.1.call-done) | copy-start | bytes 1572868
  263.6 79.6 %all-to-all-start = ((f32[16,512,128]{2,1,0:T(8,128)}), f32[16,512,128]{2,1,0:T(8,128)}, u32[]{:S(2)}, u32[]{:S(2)}) async-start(f32[16,512,128]{2,1,0:T(8,128)} %stack.2), calls=%async_computation.1 | async-start | bytes 8388608 | tf_op jit(solution)/shard_map/all_to_all | solution.py:64
  271.0 277.0 %all-reduce.4.cloned.1.call-start = ((), (), s32[]{:S(2)}) async-start(), calls=%async_computation.6 | async-start | bytes 524288 | tf_op jit(solution)/shard_map/psum | solution.py:77
  274.1 381.2 %reduce-scatter.5.cloned.1.call-start = ((), (), s32[]{:S(2)}) async-start(), calls=%async_computation.5 | async-start | bytes 4456448 | tf_op jit(solution)/shard_map/reduce_scatter | solution.py:70
Sparse Core Ops, SparseCore 0:
  10.7 111.2 all-gather.1
  158.3 100.2 reduce-scatter.2
  277.9 270.0 all-reduce.3
  552.2 103.0 reduce-scatter.4
